TPU v7x, 512 devices: a whole 4x4x16 slice. The times are simulated.
512 devices in a mesh: dp: 4 (over z_lo), row: 8 (over y, core), col: 16 (over z_hi, x).
Axes of the slice: x: 4, y: 4, z: 16 (z_hi: 4, z_lo: 4; z = z_hi * 4 + z_lo), core: 2. Of those that a mesh axis runs over, the one named last changes fastest.
Arguments:
- queries: bfloat16 [4, 64, 256, 768], P('dp', 'row', 'col'), may hold values from -5.5 to 5.5
- keys: bfloat16 [4, 64, 256, 768], P('dp', 'row', 'col'), may hold values from -5.5 to 5.5
- values: bfloat16 [4, 64, 256, 768], P('dp', 'row', 'col'), may hold values from -6 to 6
- occupancy: int32 [4, 8, 32], P('dp', 'row', 'col'), may hold values from 0 to 64, as said below
- out_weight: bfloat16 [768, 768], P('dp'), may hold values from -0.21875 to 0.21875
- grad_out: bfloat16 [4, 64, 256, 768], P('dp', 'row', 'col'), may hold values from -6 to 6
Outputs:
- grad_queries: bfloat16 [4, 64, 256, 768], P('dp', 'row', 'col')
- grad_keys: bfloat16 [4, 64, 256, 768], P('dp', 'row', 'col')
- grad_values: bfloat16 [4, 64, 256, 768], P('dp', 'row', 'col')
- grad_weight: float32 [768, 768], P('dp')
Inputs may be any that keep to these rules, and one draw needn't show every extreme that they name: `occupancy`: the occupied tiles of a block are its first that many tiles, row by row over its 8 x 8 tiles. Every slide has a block holding 8 * 8 and a block holding 0.
All inputs are finite; a program needn't handle non-finite values.
Results may differ from a plain program's by a relative error of at most 0.02.
Values may be sent and summed in bfloat16 or wider, within the bound.
A program may use at most 64 MiB of HBM per device.

v0:
```python
import jax
import jax.numpy as jnp
from jax import lax
from jax.sharding import PartitionSpec as P

HEAD_DIM = 64
SIDE = 8
REACH = 3
NEG = -1e30


def passed_along(value, axis, steps):
    count = lax.axis_size(axis)
    leading, last = (max(0, -steps), min(count, count - steps))
    return lax.ppermute(value, axis, [(source, source + steps) for source in range(leading, last)])


def for_sending(value):
    return jax.tree.map(lambda a: a.astype(jnp.bfloat16) if a.dtype == jnp.float32 else a, value)


def extended(cells, sides, width):
    for axis, dim in sides:
        count = lax.axis_size(axis)
        ends = count - 1
        head = lax.slice_in_dim(cells, 0, width, axis=dim)
        tail = lax.slice_in_dim(cells, cells.shape[dim] - width, cells.shape[dim], axis=dim)
        cells = jnp.concatenate(
            [
                lax.ppermute(tail, axis, [(i, (i + 1) % count) for i in range(ends)]),
                cells,
                lax.ppermute(head, axis, [((i + 1) % count, i) for i in range(ends)]),
            ],
            axis=dim,
        )
    return cells


def product(form, left, right):
    return jnp.einsum(form, left, right, preferred_element_type=jnp.float32)


def near_table(block_side, radius):
    window = block_side + 2 * radius
    queries_at = jnp.arange(block_side * block_side)
    keys_at = jnp.arange(window * window)
    row_gap = keys_at[None, :] // window - queries_at[:, None] // block_side - radius
    col_gap = keys_at[None, :] % window - queries_at[:, None] % block_side - radius
    return (jnp.abs(row_gap) <= radius) & (jnp.abs(col_gap) <= radius)


def tile_valid(counts, block_side):
    inside = jnp.arange(block_side * block_side, dtype=jnp.int32).reshape(block_side, block_side)
    flags = inside[None, :, None, :] < counts[:, None, :, None]
    return flags.reshape(counts.shape[0] * block_side, counts.shape[1] * block_side).astype(
        jnp.float32
    )


def blockify(source, block_side):
    height, breadth = (source.shape[0], source.shape[1])
    others = source.shape[2:]
    shaped = source.reshape(
        (height // block_side, block_side, breadth // block_side, block_side) + others
    )
    shaped = jnp.swapaxes(shaped, 1, 2)
    return shaped.reshape(
        (height // block_side, breadth // block_side, block_side * block_side) + others
    )


def unblock(source, block_side):
    block_rows, block_cols = (source.shape[0], source.shape[1])
    others = source.shape[3:]
    shaped = source.reshape((block_rows, block_cols, block_side, block_side) + others)
    shaped = jnp.swapaxes(shaped, 1, 2)
    return shaped.reshape((block_rows * block_side, block_cols * block_side) + others)


def cut_axis(source, dimension, block_side, radius, number):
    padding = [(0, 0)] * source.ndim
    padding[dimension] = (0, block_side - 2 * radius)
    shaped = jnp.pad(source, padding)
    shaped = shaped.reshape(
        source.shape[:dimension] + (number + 1, block_side) + source.shape[dimension + 1 :]
    )
    leading = lax.slice_in_dim(shaped, 0, number, axis=dimension)
    trailing = lax.slice_in_dim(
        lax.slice_in_dim(shaped, 1, number + 1, axis=dimension), 0, 2 * radius, axis=dimension + 1
    )
    return jnp.concatenate([leading, trailing], axis=dimension + 1)


def windows(source, block_side, radius, block_rows, block_cols):
    window = block_side + 2 * radius
    shaped = cut_axis(source, 0, block_side, radius, block_rows)
    shaped = cut_axis(shaped, 2, block_side, radius, block_cols)
    shaped = jnp.swapaxes(shaped, 1, 2)
    return shaped.reshape((block_rows * block_cols, window * window) + source.shape[2:])


def merge_axis(source, dimension, block_side, radius, number):
    leading = lax.slice_in_dim(source, 0, block_side, axis=dimension + 1)
    trailing = lax.slice_in_dim(source, block_side, block_side + 2 * radius, axis=dimension + 1)
    lead_pad = [(0, 0)] * source.ndim
    lead_pad[dimension] = (0, 1)
    trail_pad = [(0, 0)] * source.ndim
    trail_pad[dimension] = (1, 0)
    trail_pad[dimension + 1] = (0, block_side - 2 * radius)
    summed = jnp.pad(leading, lead_pad) + jnp.pad(trailing, trail_pad)
    summed = summed.reshape(
        source.shape[:dimension] + ((number + 1) * block_side,) + source.shape[dimension + 2 :]
    )
    return lax.slice_in_dim(summed, 0, number * block_side + 2 * radius, axis=dimension)


def fold_back(source, block_side, radius, block_rows, block_cols):
    window = block_side + 2 * radius
    shaped = source.reshape((block_rows, block_cols, window, window) + source.shape[2:])
    shaped = jnp.swapaxes(shaped, 1, 2)
    shaped = merge_axis(shaped, 2, block_side, radius, block_cols)
    return merge_axis(shaped, 0, block_side, radius, block_rows)


def attend(query_blocks, key_win, value_win, key_flag, query_flag, nearby, scaling):
    scores = product("nqhd,nkhd->nhqk", query_blocks, key_win) * scaling
    allowed = nearby[None, None] & (key_flag[:, None, None, :] > 0)
    masked = jnp.where(allowed, scores, NEG)
    highest = jnp.max(masked, axis=-1, keepdims=True)
    raised = jnp.exp(masked - highest)
    inverse = 1.0 / jnp.sum(raised, axis=-1, keepdims=True)
    weights = raised * inverse
    rounded = weights.astype(jnp.bfloat16)
    mixed = product("nhqk,nkhd->nqhd", rounded, value_win)
    attended = (mixed * query_flag[:, :, None, None]).astype(jnp.bfloat16)
    return (attended, weights, rounded, highest, inverse)


def query_side(weights, grad_blocks, key_win, value_win, scaling):
    prob_grad = product("nqhd,nkhd->nhqk", grad_blocks, value_win)
    correction = jnp.sum(weights * prob_grad, axis=-1, keepdims=True)
    score_grad = (weights * (prob_grad - correction) * scaling).astype(jnp.bfloat16)
    query_grad = product("nhqk,nkhd->nqhd", score_grad, key_win)
    return (query_grad, score_grad, correction)


def return_rims(key_full, value_full):
    middle = (key_full[REACH:-REACH], value_full[REACH:-REACH])
    for offset in (1, -1):
        if offset == 1:
            border = (key_full[-REACH:], value_full[-REACH:])
        else:
            border = (key_full[:REACH], value_full[:REACH])
        arrived = (
            passed_along(border[0].astype(jnp.bfloat16), "row", offset).astype(jnp.float32),
            passed_along(border[1].astype(jnp.bfloat16), "row", offset).astype(jnp.float32),
        )
        if offset == 1:
            middle = tuple(
                (portion.at[:REACH].add(incoming) for portion, incoming in zip(middle, arrived))
            )
        else:
            middle = tuple(
                (portion.at[-REACH:].add(incoming) for portion, incoming in zip(middle, arrived))
            )
    centre = tuple((portion[:, REACH:-REACH] for portion in middle))
    for offset in (1, -1):
        if offset == 1:
            border = tuple((portion[:, -REACH:] for portion in middle))
        else:
            border = tuple((portion[:, :REACH] for portion in middle))
        arrived = jax.tree.map(
            lambda part, own: part.astype(own.dtype),
            passed_along(for_sending(border), "col", offset),
            border,
        )
        if offset == 1:
            centre = tuple(
                (portion.at[:, :REACH].add(incoming) for portion, incoming in zip(centre, arrived))
            )
        else:
            centre = tuple(
                (portion.at[:, -REACH:].add(incoming) for portion, incoming in zip(centre, arrived))
            )
    return centre


def on_device(queries, keys, values, occupancy, out_weight, grad_out):
    query_tiles = queries[0]
    key_tiles = keys[0]
    value_tiles = values[0]
    grad_tiles = grad_out[0]
    counts = occupancy[0]
    height, breadth, channels = query_tiles.shape
    out_width = grad_tiles.shape[2]
    head_count = channels // HEAD_DIM
    block_rows = height // SIDE
    block_cols = breadth // SIDE
    block_count = block_rows * block_cols
    block_area = SIDE * SIDE
    window = SIDE + 2 * REACH
    window_area = window * window
    tile_count = height * breadth
    nearby = near_table(SIDE, REACH)
    scaling = HEAD_DIM ** (-0.5)
    occupied = tile_valid(counts, SIDE)
    key_ext, value_ext, flag_ext = (
        extended(key_tiles, (("row", 0), ("col", 1)), REACH),
        extended(value_tiles, (("row", 0), ("col", 1)), REACH),
        extended(occupied.astype(jnp.bfloat16), (("row", 0), ("col", 1)), REACH),
    )
    key_win = windows(key_ext, SIDE, REACH, block_rows, block_cols).reshape(
        block_count, window_area, head_count, HEAD_DIM
    )
    value_win = windows(value_ext, SIDE, REACH, block_rows, block_cols).reshape(
        block_count, window_area, head_count, HEAD_DIM
    )
    flag_win = windows(flag_ext, SIDE, REACH, block_rows, block_cols)
    query_blocks = blockify(query_tiles, SIDE).reshape(
        block_count, block_area, head_count, HEAD_DIM
    )
    query_flag = blockify(occupied, SIDE).reshape(block_count, block_area)
    attended, weights, rounded, highest, inverse = attend(
        query_blocks, key_win, value_win, flag_win, query_flag, nearby, scaling
    )
    flat_grads = grad_tiles.reshape(tile_count, out_width)
    out_back = lax.dot_general(
        flat_grads,
        lax.all_gather(out_weight, "dp", axis=0, tiled=True),
        (((1,), (1,)), ((), ())),
        preferred_element_type=jnp.float32,
    )
    gated_grad = out_back.astype(jnp.bfloat16).reshape(height, breadth, channels) * occupied[
        :, :, None
    ].astype(jnp.bfloat16)
    grad_blocks = blockify(gated_grad, SIDE).reshape(block_count, block_area, head_count, HEAD_DIM)
    out_blocks = blockify(grad_tiles, SIDE).reshape(tile_count, out_width)
    weight_term = lax.dot_general(
        attended.reshape(tile_count, channels),
        out_blocks,
        (((0,), (0,)), ((), ())),
        preferred_element_type=jnp.float32,
    )
    summed = lax.psum(weight_term, ("row", "col"))
    slide_part = lax.psum_scatter(
        summed.astype(jnp.bfloat16), "dp", scatter_dimension=0, tiled=True
    ).astype(jnp.float32)
    all_tiles = tile_count * lax.axis_size("dp") * lax.axis_size("row") * lax.axis_size("col")
    grad_weight = slide_part * all_tiles ** (-0.5)
    query_grad, score_grad, correction = query_side(
        weights, grad_blocks, key_win, value_win, scaling
    )
    key_part = product("nhqk,nqhd->nkhd", score_grad, query_blocks).reshape(
        block_count, window_area, channels
    )
    value_part = product("nhqk,nqhd->nkhd", rounded, grad_blocks).reshape(
        block_count, window_area, channels
    )
    key_full = fold_back(key_part, SIDE, REACH, block_rows, block_cols)
    value_full = fold_back(value_part, SIDE, REACH, block_rows, block_cols)
    key_sum, value_sum = return_rims(key_full, value_full)
    grad_query = unblock(query_grad.reshape(block_rows, block_cols, block_area, channels), SIDE)
    return (
        grad_query.astype(jnp.bfloat16)[None],
        key_sum.astype(jnp.bfloat16)[None],
        value_sum.astype(jnp.bfloat16)[None],
        grad_weight,
    )


def solution(mesh):
    return jax.shard_map(
        on_device,
        mesh=mesh,
        in_specs=(
            P("dp", "row", "col", None),
            P("dp", "row", "col", None),
            P("dp", "row", "col", None),
            P("dp", "row", "col"),
            P("dp", None),
            P("dp", "row", "col", None),
        ),
        out_specs=(
            P("dp", "row", "col", None),
            P("dp", "row", "col", None),
            P("dp", "row", "col", None),
            P("dp", None),
        ),
        check_vma=False,
    )
```

profile of v0, /device:TPU:39, one launch (start us, length us, event | category | flops | bytes accessed | tf_op | source)
XLA Modules:
  0.0 1018.1 jit_solution(9643661524782293680)
XLA Ops:
  8.3 2.6 collective-permute-start.1
  10.9 3.1 collective-permute-start
  19.8 3.6 collective-permute-start.4
  27.3 2.4 collective-permute-start.7
  29.7 8.8 collective-permute-start.6
  38.6 3.0 collective-permute-start.8
  44.1 9.4 collective-permute-start.2
  55.6 9.4 collective-permute-start.10
  66.7 9.1 collective-permute-done.11
  80.4 2.4 fusion.67
  88.0 4.9 fusion.24
  95.6 764.2 %all-reduce.15 = bf16[768,768]{1,0:T(8,128)(2,1)} all-reduce(f32[768,768]{1,0:T(8,128)S(1)} %fusion.69), channel_id=1, replica_groups=mesh['dp'=4,'row'=8,'col'=16] {'row','col'}, use_global_device_ids=true, to_apply=%region_3.4 | all-reduce | flops 589824 | bytes 3538944 | tf_op jit(solution)/shard_map/psum | solution.py:244
  864.2 11.5 %fusion.25 = bf16[2,64,12,64]{1,3,2,0:T(8,128)(2,1)} fusion(bf16[2,196,12,64]{1,3,2,0:T(8,128)(2,1)S(1)} %copy.80, f32[2,12,64,196]{3,2,1,0:T(8,128)} %fusion.68, f32[2,12,64,196]{3,2,1,0:T(8,128)} %get-tuple-element.127, f32[2,12,64]{2,1,0:T(8,128)S(1)} %broadcast_divide_fusion), kind=kOutput, calls=%fused_computation.21 | convolution fusion | flops 40742596 | bytes 3213312 | tf_op jit(solution)/shard_map/nhqk,nkhd->nqhd/dot_general | solution.py:40
  875.7 11.9 %fusion.12 = f32[2,196,12,64]{1,3,2,0:T(8,128)} fusion(bf16[2,64,12,64]{1,3,2,0:T(8,128)(2,1)S(1)} %copy-done.10, f32[2,12,64,196]{3,2,1,0:T(8,128)} %fusion.68, f32[2,12,64,196]{3,2,1,0:T(8,128)} %get-tuple-element.127, f32[2,12,64]{2,1,0:T(8,128)S(1)} %broadcast_divide_fusion), kind=kOutput, calls=%fused_computation.9 | convolution fusion | flops 40644292 | bytes 3815424 | tf_op jit(solution)/shard_map/nhqk,nqhd->nkhd/dot_general | solution.py:40
  887.7 3.5 copy.84
  897.9 5.8 convolution_bitcast_fusion
  903.7 3.5 copy.87
  917.1 51.0 %collective-permute-start.13 = (bf16[3,22,768]{2,1,0:T(8,128)(2,1)S(1)}, bf16[3,22,768]{2,1,0:T(8,128)(2,1)S(1)}, u32[]{:S(2)}, u32[]{:S(2)}) collective-permute-start(bf16[3,22,768]{2,1,0:T(8,128)(2,1)S(1)} %get-tuple-element.102), channel_id=1, source_target_pairs={{16,0},{32,16},{48,32},{64,48},{80,64},{96,80},{112,96},{17,1},{33... | collective-permute-start | bytes 304136 | tf_op jit(solution)/shard_map/ppermute | solution.py:15
  970.0 2.4 collective-permute-start.17
  972.7 3.4 collective-permute-done.17
  976.3 9.0 collective-permute-start.14
  985.3 3.1 collective-permute-start.15
  988.5 8.2 collective-permute-start.18
  999.8 7.9 collective-permute-done.19
  (182 shorter events, 58.9 us)
Async XLA Ops:
  7.2 852.7 %all-gather.2.cloned.1.call-start = ((), (), s32[]{:S(2)}) async-start(), calls=%async_computation.1 | async-start | bytes 1474560 | tf_op jit(solution)/shard_map/all_gather | solution.py:229
  8.3 33.8 %collective-permute-start.1 = (bf16[3,16,768]{2,1,0:T(8,128)(2,1)S(1)}, bf16[3,16,768]{2,1,0:T(8,128)(2,1)S(1)}, u32[]{:S(2)}, u32[]{:S(2)}) collective-permute-start(bf16[3,16,768]{2,1,0:T(8,128)(2,1)S(1)} %get-tuple-element.119), channel_id=1, source_target_pairs={{16,0},{32,16},{48,32},{64,48},{80,64},{96,80},{112,96},{17,1},{33... | collective-permute-start | bytes 221192 | tf_op jit(solution)/shard_map/ppermute | solution.py:32
  10.9 31.2 %collective-permute-start = (bf16[3,16,768]{2,1,0:T(8,128)(2,1)S(1)}, bf16[3,16,768]{2,1,0:T(8,128)(2,1)S(1)}, u32[]{:S(2)}, u32[]{:S(2)}) collective-permute-start(bf16[3,16,768]{2,1,0:T(8,128)(2,1)S(1)} %get-tuple-element.118), channel_id=1, source_target_pairs={{0,16},{16,32},{32,48},{48,64},{64,80},{80,96},{96,112},{1,17},{17... | collective-permute-start | bytes 221192 | tf_op jit(solution)/shard_map/ppermute | solution.py:30
  14.0 995.5 %reduce-scatter.2.cloned.1.call-start = ((), (), s32[]{:S(2)}) async-start(), calls=%async_computation.2 | async-start | bytes 1474560 | tf_op jit(solution)/shard_map/reduce_scatter | solution.py:245
  15.0 38.5 %collective-permute-start.9 = (bf16[3,16,768]{2,1,0:T(8,128)(2,1)S(1)}, bf16[3,16,768]{2,1,0:T(8,128)(2,1)S(1)}, u32[]{:S(2)}, u32[]{:S(2)}) collective-permute-start(bf16[3,16,768]{2,1,0:T(8,128)(2,1)S(1)} %get-tuple-element.117), channel_id=1, source_target_pairs={{16,0},{32,16},{48,32},{64,48},{80,64},{96,80},{112,96},{17,1},{33... | collective-permute-start | bytes 221192 | tf_op jit(solution)/shard_map/ppermute | solution.py:32
  17.9 9.3 collective-permute-start.5
  19.8 7.4 collective-permute-start.4
  26.3 56.6 %copy-start.9 = (bf16[2,64,12,64]{1,3,2,0:T(8,128)(2,1)}, bf16[2,64,12,64]{1,3,2,0:T(8,128)(2,1)S(1)}, u32[]{:S(2)}) copy-start(bf16[2,64,12,64]{1,3,2,0:T(8,128)(2,1)S(1)} %copy.83) | copy-start | bytes 589828
  27.3 11.3 %collective-permute-start.7 = (bf16[14,3]{1,0:T(8,128)(2,1)S(1)}, bf16[14,3]{1,0:T(8,128)(2,1)S(1)}, u32[]{:S(2)}, u32[]{:S(2)}) collective-permute-start(bf16[14,3]{1,0:T(8,128)(2,1)S(1)} %get-tuple-element.123), channel_id=1, source_target_pairs={{1,0},{2,1},{3,2},{4,3},{5,4},{6,5},{7,6},{8,7},{9,8},{10,9},{11,1... | collective-permute-start | bytes 260 | tf_op jit(solution)/shard_map/ppermute | solution.py:32
  29.7 11.8 %collective-permute-start.6 = (bf16[14,3]{1,0:T(8,128)(2,1)S(1)}, bf16[14,3]{1,0:T(8,128)(2,1)S(1)}, u32[]{:S(2)}, u32[]{:S(2)}) collective-permute-start(bf16[14,3]{1,0:T(8,128)(2,1)S(1)} %get-tuple-element.122), channel_id=1, source_target_pairs={{0,1},{1,2},{2,3},{3,4},{4,5},{5,6},{6,7},{7,8},{8,9},{9,10},{10,1... | collective-permute-start | bytes 260 | tf_op jit(solution)/shard_map/ppermute | solution.py:30
  38.6 14.9 %collective-permute-start.8 = (bf16[3,16,768]{2,1,0:T(8,128)(2,1)S(1)}, bf16[3,16,768]{2,1,0:T(8,128)(2,1)S(1)}, u32[]{:S(2)}, u32[]{:S(2)}) collective-permute-start(bf16[3,16,768]{2,1,0:T(8,128)(2,1)S(1)} %get-tuple-element.116), channel_id=1, source_target_pairs={{0,16},{16,32},{32,48},{48,64},{64,80},{80,96},{96,112},{1,17},{17... | collective-permute-start | bytes 221192 | tf_op jit(solution)/shard_map/ppermute | solution.py:30
  42.2 24.1 %collective-permute-start.3 = (bf16[14,3,768]{2,1,0:T(4,128)(2,1)S(1)}, bf16[14,3,768]{2,1,0:T(4,128)(2,1)S(1)}, u32[]{:S(2)}, u32[]{:S(2)}) collective-permute-start(bf16[14,3,768]{2,1,0:T(4,128)(2,1)S(1)} %get-tuple-element.111), channel_id=1, source_target_pairs={{1,0},{2,1},{3,2},{4,3},{5,4},{6,5},{7,6},{8,7},{9,8},{10,9},{11,1... | collective-permute-start | bytes 193544 | tf_op jit(solution)/shard_map/ppermute | solution.py:32
  44.1 22.2 %collective-permute-start.2 = (bf16[14,3,768]{2,1,0:T(4,128)(2,1)S(1)}, bf16[14,3,768]{2,1,0:T(4,128)(2,1)S(1)}, u32[]{:S(2)}, u32[]{:S(2)}) collective-permute-start(bf16[14,3,768]{2,1,0:T(4,128)(2,1)S(1)} %get-tuple-element.110), channel_id=1, source_target_pairs={{0,1},{1,2},{2,3},{3,4},{4,5},{5,6},{6,7},{7,8},{8,9},{9,10},{10,1... | collective-permute-start | bytes 193544 | tf_op jit(solution)/shard_map/ppermute | solution.py:30
  53.6 22.2 %collective-permute-start.11 = (bf16[14,3,768]{2,1,0:T(4,128)(2,1)S(1)}, bf16[14,3,768]{2,1,0:T(4,128)(2,1)S(1)}, u32[]{:S(2)}, u32[]{:S(2)}) collective-permute-start(bf16[14,3,768]{2,1,0:T(4,128)(2,1)S(1)} %get-tuple-element.109), channel_id=1, source_target_pairs={{1,0},{2,1},{3,2},{4,3},{5,4},{6,5},{7,6},{8,7},{9,8},{10,9},{11,1... | collective-permute-start | bytes 193544 | tf_op jit(solution)/shard_map/ppermute | solution.py:32
  55.6 20.3 %collective-permute-start.10 = (bf16[14,3,768]{2,1,0:T(4,128)(2,1)S(1)}, bf16[14,3,768]{2,1,0:T(4,128)(2,1)S(1)}, u32[]{:S(2)}, u32[]{:S(2)}) collective-permute-start(bf16[14,3,768]{2,1,0:T(4,128)(2,1)S(1)} %get-tuple-element.108), channel_id=1, source_target_pairs={{0,1},{1,2},{2,3},{3,4},{4,5},{5,6},{6,7},{7,8},{8,9},{9,10},{10,1... | collective-permute-start | bytes 193544 | tf_op jit(solution)/shard_map/ppermute | solution.py:30
  95.6 764.3 %copy-start.15 = (bf16[1,8,16,768]{3,2,1,0:T(8,128)(2,1)S(1)}, bf16[1,8,16,768]{3,2,1,0:T(8,128)(2,1)}, u32[]{:S(2)}) copy-start(bf16[1,8,16,768]{3,2,1,0:T(8,128)(2,1)} %param.27) | copy-start | bytes 589828
  914.9 57.5 %collective-permute-start.12 = (bf16[3,22,768]{2,1,0:T(8,128)(2,1)S(1)}, bf16[3,22,768]{2,1,0:T(8,128)(2,1)S(1)}, u32[]{:S(2)}, u32[]{:S(2)}) collective-permute-start(bf16[3,22,768]{2,1,0:T(8,128)(2,1)S(1)} %get-tuple-element.103), channel_id=1, source_target_pairs={{0,16},{16,32},{32,48},{48,64},{64,80},{80,96},{96,112},{1,17},{17... | collective-permute-start | bytes 304136 | tf_op jit(solution)/shard_map/ppermute | solution.py:15
  917.1 55.4 %collective-permute-start.13 = (bf16[3,22,768]{2,1,0:T(8,128)(2,1)S(1)}, bf16[3,22,768]{2,1,0:T(8,128)(2,1)S(1)}, u32[]{:S(2)}, u32[]{:S(2)}) collective-permute-start(bf16[3,22,768]{2,1,0:T(8,128)(2,1)S(1)} %get-tuple-element.102), channel_id=1, source_target_pairs={{16,0},{32,16},{48,32},{64,48},{80,64},{96,80},{112,96},{17,1},{33... | collective-permute-start | bytes 304136 | tf_op jit(solution)/shard_map/ppermute | solution.py:15
  968.1 4.4 collective-permute-start.16
  970.0 6.1 collective-permute-start.17
  976.3 22.3 %collective-permute-start.14 = (bf16[8,3,768]{2,1,0:T(4,128)(2,1)S(1)}, bf16[8,3,768]{2,1,0:T(4,128)(2,1)S(1)}, u32[]{:S(2)}, u32[]{:S(2)}) collective-permute-start(bf16[8,3,768]{2,1,0:T(4,128)(2,1)S(1)} %get-tuple-element.115), channel_id=1, source_target_pairs={{0,1},{1,2},{2,3},{3,4},{4,5},{5,6},{6,7},{7,8},{8,9},{9,10},{10,1... | collective-permute-start | bytes 110600 | tf_op jit(solution)/shard_map/ppermute | solution.py:15
  985.3 13.8 %collective-permute-start.15 = (bf16[8,3,768]{2,1,0:T(4,128)(2,1)S(1)}, bf16[8,3,768]{2,1,0:T(4,128)(2,1)S(1)}, u32[]{:S(2)}, u32[]{:S(2)}) collective-permute-start(bf16[8,3,768]{2,1,0:T(4,128)(2,1)S(1)} %get-tuple-element.114), channel_id=1, source_target_pairs={{1,0},{2,1},{3,2},{4,3},{5,4},{6,5},{7,6},{8,7},{9,8},{10,9},{11,1... | collective-permute-start | bytes 110600 | tf_op jit(solution)/shard_map/ppermute | solution.py:15
  988.5 10.2 collective-permute-start.18
  996.7 11.1 %collective-permute-start.19 = (bf16[8,3,768]{2,1,0:T(4,128)(2,1)S(1)}, bf16[8,3,768]{2,1,0:T(4,128)(2,1)S(1)}, u32[]{:S(2)}, u32[]{:S(2)}) collective-permute-start(bf16[8,3,768]{2,1,0:T(4,128)(2,1)S(1)} %get-tuple-element.112), channel_id=1, source_target_pairs={{1,0},{2,1},{3,2},{4,3},{5,4},{6,5},{7,6},{8,7},{9,8},{10,9},{11,1... | collective-permute-start | bytes 110600 | tf_op jit(solution)/shard_map/ppermute | solution.py:15
  (19 other events, 153.0 us)
Sparse Core Ops, SparseCore 0:
  14.1 41.7 all-gather.1
  860.0 89.8 reduce-scatter.1
where the time goes:
time: 1020 us
  blocking collectives  764 us (75%)
  starting transfers between devices  130 us (13%)
  matrix products  43 us (4%)
  local copies, waits for them, and re-layouts  35 us (3%)
  waiting for transfers between devices  21.9 us (2%)
  between operations  15.1 us (1%)
    psum x1, blocking collectives, on_device(): summed = lax.psum(weight_term, ('row', 'col'))  764 us
    ppermute x8, starting transfers between devices, passed_along(): lax.ppermute(value, axis, [(source, source + steps) for source in range(l...  79.4 us
    ppermute x6, starting transfers between devices, extended(): lax.ppermute(tail, axis, [(i, (i + 1) % count) for i in range(ends)])  37.3 us
    dot_general x6, matrix products, product(): return jnp.einsum(form, left, right, preferred_element_type=jnp.float32)  37.2 us
  transfers between devices with their start and end apart: 22, of which 4 were waited for; matrix products, arithmetic and copies ran while one was open for 8% of the time, Pallas kernels for 0%

commit v1 on v0

--- a/solution.py
+++ b/solution.py
@@ -241,7 +241,7 @@
         (((0,), (0,)), ((), ())),
         preferred_element_type=jnp.float32,
     )
-    summed = lax.psum(weight_term, ("row", "col"))
+    summed = lax.psum(lax.psum(weight_term, axis_name="col"), axis_name="row")
     slide_part = lax.psum_scatter(
         summed.astype(jnp.bfloat16), "dp", scatter_dimension=0, tiled=True
     ).astype(jnp.float32)

time: 1020 us -> 479 us (0.47)
  the two profiles are of different devices: /device:TPU:39 before, /device:TPU:1 now
where the time goes in v1:
time: 479 us; the launch traced here: 478 us
  waiting for transfers between devices  256 us (53%)
  blocking collectives  62.1 us (13%)
  starting transfers between devices  56.4 us (12%)
  matrix products  39.4 us (8%)
  local copies, waits for them, and re-layouts  37.4 us (8%)
  between operations  16.5 us (3%)
  other arithmetic  9.72 us (2%)
    psum x1, waiting for transfers between devices, on_device(): summed = lax.psum(lax.psum(weight_term, axis_name='col'), axis_name='row')  228 us
    psum x1, blocking collectives, on_device(): summed = lax.psum(lax.psum(weight_term, axis_name='col'), axis_name='row')  62.1 us
    dot_general x6, matrix products, product(): return jnp.einsum(form, left, right, preferred_element_type=jnp.float32)  32.8 us
    reduce_scatter x1, waiting for transfers between devices, on_device(): lax.psum_scatter(summed.astype(jnp.bfloat16), 'dp', scatter_dimension=0,...  24.9 us
    ppermute x6, starting transfers between devices, extended(): lax.ppermute(tail, axis, [(i, (i + 1) % count) for i in range(ends)])  20 us
    ppermute x8, starting transfers between devices, passed_along(): lax.ppermute(value, axis, [(source, source + steps) for source in range(l...  19.2 us
    ppermute x6, starting transfers between devices, extended(): lax.ppermute(head, axis, [((i + 1) % count, i) for i in range(ends)])  16.9 us
  transfers between devices with their start and end apart: 23, of which 4 were waited for; matrix products, arithmetic and copies ran while one was open for 17% of the time, Pallas kernels for 0%

profile of v1, /device:TPU:1, one launch (start us, length us, event | category | flops | bytes accessed | tf_op | source)
XLA Modules:
  0.0 477.6 jit_solution(6057512787554124429)
XLA Ops:
  9.1 8.7 %collective-permute-start.1 = (bf16[3,16,768]{2,1,0:T(8,128)(2,1)S(1)}, bf16[3,16,768]{2,1,0:T(8,128)(2,1)S(1)}, u32[]{:S(2)}, u32[]{:S(2)}) collective-permute-start(bf16[3,16,768]{2,1,0:T(8,128)(2,1)S(1)} %get-tuple-element.119), channel_id=1, source_target_pairs={{16,0},{32,16},{48,32},{64,48},{80,64},{96,80},{112,96},{17,1},{33... | collective-permute-start | bytes 221192 | tf_op jit(solution)/shard_map/ppermute | solution.py:32
  20.8 2.4 collective-permute-start.9
  26.1 3.6 collective-permute-start.4
  35.0 4.0 collective-permute-start.6
  39.0 2.5 collective-permute-start.8
  43.4 4.0 collective-permute-start.2
  48.8 4.0 collective-permute-start.10
  61.7 2.9 fusion.67
  66.1 3.5 fusion.24
  78.3 10.9 %fusion.12 = f32[2,196,12,64]{1,3,2,0:T(8,128)} fusion(bf16[2,64,12,64]{1,3,2,0:T(8,128)(2,1)S(1)} %copy-done.11, f32[2,12,64,196]{3,2,1,0:T(8,128)S(1)} %fusion.68, f32[2,12,64,196]{3,2,1,0:T(8,128)} %get-tuple-element.127, f32[2,12,64]{2,1,0:T(8,128)S(1)} %broadcast_divide_fusion), kind=kOutput, calls=%fused_computation.9 | convolution fusion | flops 40644292 | bytes 3815424 | tf_op jit(solution)/shard_map/nhqk,nqhd->nkhd/dot_general | solution.py:40
  89.2 3.5 copy.84
  92.7 2.2 reshape_reshape.26
  99.5 5.8 %convolution_bitcast_fusion = f32[2,196,12,64]{1,3,2,0:T(8,128)} fusion(bf16[2,64,12,64]{1,3,2,0:T(8,128)(2,1)S(1)} %copy-done.2, f32[2,12,64]{2,1,0:T(8,128)S(1)} %broadcast_divide_fusion, f32[2,12,64,196]{3,2,1,0:T(8,128)} %copy-done.7), kind=kOutput, calls=%fused_computation.11 | convolution fusion | flops 39440068 | bytes 2611200 | tf_op jit(solution)/shard_map/nhqk,nqhd->nkhd/dot_general | solution.py:40
  105.3 3.5 copy.87
  108.8 2.2 reshape_reshape.27
  115.2 10.7 %fusion.25 = bf16[2,64,12,64]{1,3,2,0:T(8,128)(2,1)S(1)} fusion(bf16[2,196,12,64]{1,3,2,0:T(8,128)(2,1)S(1)} %copy-done.4, f32[2,12,64,196]{3,2,1,0:T(8,128)} %copy-done.10, f32[2,12,64,196]{3,2,1,0:T(8,128)} %get-tuple-element.127, f32[2,12,64]{2,1,0:T(8,128)S(1)} %broadcast_divide_fusion), kind=kOutput, calls=%fused_computation.21 | convolution fusion | flops 40742596 | bytes 3213312 | tf_op jit(solution)/shard_map/nhqk,nkhd->nqhd/dot_general | solution.py:40
  127.0 3.8 collective-permute-start.12
  130.8 1.9 collective-permute-start.13
  133.7 3.6 collective-permute-start.16
  139.3 227.5 %all-reduce.17.cloned.1.call-done = f32[768,768]{1,0:T(8,128)} async-done(((f32[768,768]{1,0:T(8,128)}), f32[768,768]{1,0:T(8,128)}) %all-reduce.17.cloned.1.call-update) | async-done | bytes 2359312 | tf_op jit(solution)/shard_map/psum | solution.py:244
  366.8 62.1 %all-reduce.18 = bf16[768,768]{1,0:T(8,128)(2,1)} all-reduce(f32[768,768]{1,0:T(8,128)} %all-reduce.17.cloned.1.call-done), channel_id=1, replica_groups=mesh['dp'=4,'row'=8,'col'=16] {'row'}, use_global_device_ids=true, to_apply=%region_4.5 | all-reduce | flops 589824 | bytes 3538944 | tf_op jit(solution)/shard_map/psum | solution.py:244
  432.9 4.0 collective-permute-start.18
  439.4 2.3 collective-permute-done.19
  443.4 24.9 %reduce-scatter.2.cloned.1.call-done = bf16[192,768]{1,0:T(8,128)(2,1)} async-done(((bf16[768,768]{1,0:T(8,128)(2,1)}), bf16[192,768]{1,0:T(8,128)(2,1)}) %reduce-scatter.2.cloned.1.call-update) | async-done | bytes 294928 | tf_op jit(solution)/shard_map/reduce_scatter | solution.py:245
  (180 shorter events, 56.4 us)
Async XLA Ops:
  8.0 24.9 %copy-start.14 = (bf16[1,8,16,768]{3,2,1,0:T(8,128)(2,1)S(1)}, bf16[1,8,16,768]{3,2,1,0:T(8,128)(2,1)}, u32[]{:S(2)}) copy-start(bf16[1,8,16,768]{3,2,1,0:T(8,128)(2,1)} %param.27) | copy-start | bytes 589828
  8.0 65.3 %all-gather.2.cloned.1.call-start = ((), (), s32[]{:S(2)}) async-start(), calls=%async_computation.1 | async-start | bytes 1474560 | tf_op jit(solution)/shard_map/all_gather | solution.py:229
  9.1 32.9 %collective-permute-start.1 = (bf16[3,16,768]{2,1,0:T(8,128)(2,1)S(1)}, bf16[3,16,768]{2,1,0:T(8,128)(2,1)S(1)}, u32[]{:S(2)}, u32[]{:S(2)}) collective-permute-start(bf16[3,16,768]{2,1,0:T(8,128)(2,1)S(1)} %get-tuple-element.119), channel_id=1, source_target_pairs={{16,0},{32,16},{48,32},{64,48},{80,64},{96,80},{112,96},{17,1},{33... | collective-permute-start | bytes 221192 | tf_op jit(solution)/shard_map/ppermute | solution.py:32
  17.9 24.2 %collective-permute-start = (bf16[3,16,768]{2,1,0:T(8,128)(2,1)S(1)}, bf16[3,16,768]{2,1,0:T(8,128)(2,1)S(1)}, u32[]{:S(2)}, u32[]{:S(2)}) collective-permute-start(bf16[3,16,768]{2,1,0:T(8,128)(2,1)S(1)} %get-tuple-element.118), channel_id=1, source_target_pairs={{0,16},{16,32},{32,48},{48,64},{64,80},{80,96},{96,112},{1,17},{17... | collective-permute-start | bytes 221192 | tf_op jit(solution)/shard_map/ppermute | solution.py:30
  19.8 347.0 %all-reduce.17.cloned.1.call-start = ((), (), s32[]{:S(2)}) async-start(), calls=%async_computation.2 | async-start | bytes 4718592 | tf_op jit(solution)/shard_map/psum | solution.py:244
  20.8 26.6 %collective-permute-start.9 = (bf16[3,16,768]{2,1,0:T(8,128)(2,1)S(1)}, bf16[3,16,768]{2,1,0:T(8,128)(2,1)S(1)}, u32[]{:S(2)}, u32[]{:S(2)}) collective-permute-start(bf16[3,16,768]{2,1,0:T(8,128)(2,1)S(1)} %get-tuple-element.117), channel_id=1, source_target_pairs={{16,0},{32,16},{48,32},{64,48},{80,64},{96,80},{112,96},{17,1},{33... | collective-permute-start | bytes 221192 | tf_op jit(solution)/shard_map/ppermute | solution.py:32
  24.2 9.4 %collective-permute-start.5 = (bf16[3,16]{1,0:T(4,128)(2,1)S(1)}, bf16[3,16]{1,0:T(4,128)(2,1)S(1)}, u32[]{:S(2)}, u32[]{:S(2)}) collective-permute-start(bf16[3,16]{1,0:T(4,128)(2,1)S(1)} %get-tuple-element.125), channel_id=1, source_target_pairs={{16,0},{32,16},{48,32},{64,48},{80,64},{96,80},{112,96},{17,1},{33... | collective-permute-start | bytes 296 | tf_op jit(solution)/shard_map/ppermute | solution.py:32
  26.1 7.5 %collective-permute-start.4 = (bf16[3,16]{1,0:T(4,128)(2,1)S(1)}, bf16[3,16]{1,0:T(4,128)(2,1)S(1)}, u32[]{:S(2)}, u32[]{:S(2)}) collective-permute-start(bf16[3,16]{1,0:T(4,128)(2,1)S(1)} %get-tuple-element.124), channel_id=1, source_target_pairs={{0,16},{16,32},{32,48},{48,64},{64,80},{80,96},{96,112},{1,17},{17... | collective-permute-start | bytes 296 | tf_op jit(solution)/shard_map/ppermute | solution.py:30
  33.7 5.3 %collective-permute-start.7 = (bf16[14,3]{1,0:T(8,128)(2,1)S(1)}, bf16[14,3]{1,0:T(8,128)(2,1)S(1)}, u32[]{:S(2)}, u32[]{:S(2)}) collective-permute-start(bf16[14,3]{1,0:T(8,128)(2,1)S(1)} %get-tuple-element.123), channel_id=1, source_target_pairs={{1,0},{2,1},{3,2},{4,3},{5,4},{6,5},{7,6},{8,7},{9,8},{10,9},{11,1... | collective-permute-start | bytes 260 | tf_op jit(solution)/shard_map/ppermute | solution.py:32
  35.0 6.5 %collective-permute-start.6 = (bf16[14,3]{1,0:T(8,128)(2,1)S(1)}, bf16[14,3]{1,0:T(8,128)(2,1)S(1)}, u32[]{:S(2)}, u32[]{:S(2)}) collective-permute-start(bf16[14,3]{1,0:T(8,128)(2,1)S(1)} %get-tuple-element.122), channel_id=1, source_target_pairs={{0,1},{1,2},{2,3},{3,4},{4,5},{5,6},{6,7},{7,8},{8,9},{9,10},{10,1... | collective-permute-start | bytes 260 | tf_op jit(solution)/shard_map/ppermute | solution.py:30
  39.0 8.4 %collective-permute-start.8 = (bf16[3,16,768]{2,1,0:T(8,128)(2,1)S(1)}, bf16[3,16,768]{2,1,0:T(8,128)(2,1)S(1)}, u32[]{:S(2)}, u32[]{:S(2)}) collective-permute-start(bf16[3,16,768]{2,1,0:T(8,128)(2,1)S(1)} %get-tuple-element.116), channel_id=1, source_target_pairs={{0,16},{16,32},{32,48},{48,64},{64,80},{80,96},{96,112},{1,17},{17... | collective-permute-start | bytes 221192 | tf_op jit(solution)/shard_map/ppermute | solution.py:30
  42.1 10.7 %collective-permute-start.3 = (bf16[14,3,768]{2,1,0:T(4,128)(2,1)S(1)}, bf16[14,3,768]{2,1,0:T(4,128)(2,1)S(1)}, u32[]{:S(2)}, u32[]{:S(2)}) collective-permute-start(bf16[14,3,768]{2,1,0:T(4,128)(2,1)S(1)} %get-tuple-element.111), channel_id=1, source_target_pairs={{1,0},{2,1},{3,2},{4,3},{5,4},{6,5},{7,6},{8,7},{9,8},{10,9},{11,1... | collective-permute-start | bytes 193544 | tf_op jit(solution)/shard_map/ppermute | solution.py:32
  43.4 9.4 %collective-permute-start.2 = (bf16[14,3,768]{2,1,0:T(4,128)(2,1)S(1)}, bf16[14,3,768]{2,1,0:T(4,128)(2,1)S(1)}, u32[]{:S(2)}, u32[]{:S(2)}) collective-permute-start(bf16[14,3,768]{2,1,0:T(4,128)(2,1)S(1)} %get-tuple-element.110), channel_id=1, source_target_pairs={{0,1},{1,2},{2,3},{3,4},{4,5},{5,6},{6,7},{7,8},{8,9},{9,10},{10,1... | collective-permute-start | bytes 193544 | tf_op jit(solution)/shard_map/ppermute | solution.py:30
  47.5 5.6 %collective-permute-start.11 = (bf16[14,3,768]{2,1,0:T(4,128)(2,1)S(1)}, bf16[14,3,768]{2,1,0:T(4,128)(2,1)S(1)}, u32[]{:S(2)}, u32[]{:S(2)}) collective-permute-start(bf16[14,3,768]{2,1,0:T(4,128)(2,1)S(1)} %get-tuple-element.109), channel_id=1, source_target_pairs={{1,0},{2,1},{3,2},{4,3},{5,4},{6,5},{7,6},{8,7},{9,8},{10,9},{11,1... | collective-permute-start | bytes 193544 | tf_op jit(solution)/shard_map/ppermute | solution.py:32
  48.8 5.5 %collective-permute-start.10 = (bf16[14,3,768]{2,1,0:T(4,128)(2,1)S(1)}, bf16[14,3,768]{2,1,0:T(4,128)(2,1)S(1)}, u32[]{:S(2)}, u32[]{:S(2)}) collective-permute-start(bf16[14,3,768]{2,1,0:T(4,128)(2,1)S(1)} %get-tuple-element.108), channel_id=1, source_target_pairs={{0,1},{1,2},{2,3},{3,4},{4,5},{5,6},{6,7},{7,8},{8,9},{9,10},{10,1... | collective-permute-start | bytes 193544 | tf_op jit(solution)/shard_map/ppermute | solution.py:30
  73.1 395.3 %reduce-scatter.2.cloned.1.call-start = ((), (), s32[]{:S(2)}) async-start(), calls=%async_computation.3 | async-start | bytes 1474560 | tf_op jit(solution)/shard_map/reduce_scatter | solution.py:245
  127.0 12.3 %collective-permute-start.12 = (bf16[3,22,768]{2,1,0:T(8,128)(2,1)S(1)}, bf16[3,22,768]{2,1,0:T(8,128)(2,1)S(1)}, u32[]{:S(2)}, u32[]{:S(2)}) collective-permute-start(bf16[3,22,768]{2,1,0:T(8,128)(2,1)S(1)} %get-tuple-element.103), channel_id=1, source_target_pairs={{0,16},{16,32},{32,48},{48,64},{64,80},{80,96},{96,112},{1,17},{17... | collective-permute-start | bytes 304136 | tf_op jit(solution)/shard_map/ppermute | solution.py:15
  130.8 298.1 %collective-permute-start.13 = (bf16[3,22,768]{2,1,0:T(8,128)(2,1)S(1)}, bf16[3,22,768]{2,1,0:T(8,128)(2,1)}, u32[]{:S(2)}, u32[]{:S(2)}) collective-permute-start(bf16[3,22,768]{2,1,0:T(8,128)(2,1)S(1)} %get-tuple-element.102), channel_id=1, source_target_pairs={{16,0},{32,16},{48,32},{64,48},{80,64},{96,80},{112,96},{17,1},{33... | collective-permute-start | bytes 304136 | tf_op jit(solution)/shard_map/ppermute | solution.py:15
  133.7 296.2 %collective-permute-start.16 = (bf16[3,22,768]{2,1,0:T(8,128)(2,1)S(1)}, bf16[3,22,768]{2,1,0:T(8,128)(2,1)S(1)}, u32[]{:S(2)}, u32[]{:S(2)}) collective-permute-start(bf16[3,22,768]{2,1,0:T(8,128)(2,1)S(1)} %get-tuple-element.101), channel_id=1, source_target_pairs={{0,16},{16,32},{32,48},{48,64},{64,80},{80,96},{96,112},{1,17},{17... | collective-permute-start | bytes 304136 | tf_op jit(solution)/shard_map/ppermute | solution.py:15
  137.3 292.7 %collective-permute-start.17 = (bf16[3,22,768]{2,1,0:T(8,128)(2,1)S(1)}, bf16[3,22,768]{2,1,0:T(8,128)(2,1)S(1)}, u32[]{:S(2)}, u32[]{:S(2)}) collective-permute-start(bf16[3,22,768]{2,1,0:T(8,128)(2,1)S(1)} %get-tuple-element.100), channel_id=1, source_target_pairs={{16,0},{32,16},{48,32},{64,48},{80,64},{96,80},{112,96},{17,1},{33... | collective-permute-start | bytes 304136 | tf_op jit(solution)/shard_map/ppermute | solution.py:15
  430.2 8.0 %collective-permute-start.14 = (bf16[8,3,768]{2,1,0:T(4,128)(2,1)S(1)}, bf16[8,3,768]{2,1,0:T(4,128)(2,1)S(1)}, u32[]{:S(2)}, u32[]{:S(2)}) collective-permute-start(bf16[8,3,768]{2,1,0:T(4,128)(2,1)S(1)} %get-tuple-element.115), channel_id=1, source_target_pairs={{0,1},{1,2},{2,3},{3,4},{4,5},{5,6},{6,7},{7,8},{8,9},{9,10},{10,1... | collective-permute-start | bytes 110600 | tf_op jit(solution)/shard_map/ppermute | solution.py:15
  431.5 7.1 %collective-permute-start.15 = (bf16[8,3,768]{2,1,0:T(4,128)(2,1)S(1)}, bf16[8,3,768]{2,1,0:T(4,128)(2,1)S(1)}, u32[]{:S(2)}, u32[]{:S(2)}) collective-permute-start(bf16[8,3,768]{2,1,0:T(4,128)(2,1)S(1)} %get-tuple-element.114), channel_id=1, source_target_pairs={{1,0},{2,1},{3,2},{4,3},{5,4},{6,5},{7,6},{8,7},{9,8},{10,9},{11,1... | collective-permute-start | bytes 110600 | tf_op jit(solution)/shard_map/ppermute | solution.py:15
  432.9 5.4 %collective-permute-start.18 = (bf16[8,3,768]{2,1,0:T(4,128)(2,1)S(1)}, bf16[8,3,768]{2,1,0:T(4,128)(2,1)S(1)}, u32[]{:S(2)}, u32[]{:S(2)}) collective-permute-start(bf16[8,3,768]{2,1,0:T(4,128)(2,1)S(1)} %get-tuple-element.113), channel_id=1, source_target_pairs={{0,1},{1,2},{2,3},{3,4},{4,5},{5,6},{6,7},{7,8},{8,9},{9,10},{10,1... | collective-permute-start | bytes 110600 | tf_op jit(solution)/shard_map/ppermute | solution.py:15
  436.9 4.8 %collective-permute-start.19 = (bf16[8,3,768]{2,1,0:T(4,128)(2,1)S(1)}, bf16[8,3,768]{2,1,0:T(4,128)(2,1)S(1)}, u32[]{:S(2)}, u32[]{:S(2)}) collective-permute-start(bf16[8,3,768]{2,1,0:T(4,128)(2,1)S(1)} %get-tuple-element.112), channel_id=1, source_target_pairs={{1,0},{2,1},{3,2},{4,3},{5,4},{6,5},{7,6},{8,7},{9,8},{10,9},{11,1... | collective-permute-start | bytes 110600 | tf_op jit(solution)/shard_map/ppermute | solution.py:15
  (17 other events, 117.1 us)
Sparse Core Ops, SparseCore 0:
  19.9 43.1 all-gather.1
  429.1 39.2 reduce-scatter.1
Sparse Core Ops, SparseCore 1:
  73.2 293.6 all-reduce.16
